TPU v7x, 32 devices: a whole 2x2x4 slice. The times are simulated.
32 devices in a mesh: groups: 2 (over y), shot: 4 (over x, core), slab: 4 (over z).
Axes of the slice: x: 2, y: 2, z: 4, core: 2. Of those that a mesh axis runs over, the one named last changes fastest.
Arguments:
- slowness: float32 [32, 192, 128], P(('groups', 'slab')), parts along dimension 0, may hold values from 0.8 to 1.25
- wave_prev: float32 [8, 16, 192, 128], P(('groups', 'shot'), 'slab'), parts along dimension 0, may hold values from -6 to 6
- wave_now: float32 [8, 16, 192, 128], P(('groups', 'shot'), 'slab'), parts along dimension 0, may hold values from -6 to 6
- memory: float32 [8, 3, 16, 192, 128], P(('groups', 'shot'), None, 'slab'), parts along dimension 0, may hold values from -6 to 6
- adjoint_now: float32 [8, 16, 192, 128], P(('groups', 'shot'), 'slab'), parts along dimension 0, may hold values from -6 to 6
- adjoint_prev: float32 [8, 16, 192, 128], P(('groups', 'shot'), 'slab'), parts along dimension 0, may hold values from -6 to 6
- wavelet: float32 [4], replicated, may hold values from -16 to 16
- src_cells: int32 [8, 64], P(('groups', 'shot')), parts along dimension 0, may hold values from 0 to 393215
- src_signs: int32 [8, 64], P(('groups', 'shot')), parts along dimension 0, may hold values from -1 to 1, as said below
- rec_cells: int32 [512], P('groups'), parts along dimension 0, may hold values from 0 to 393215
- observed: float32 [8, 4, 256], P(('groups', 'shot')), parts along dimension 0, may hold values from -6 to 6
Outputs:
- new_slowness: float32 [32, 192, 128], P(('groups', 'slab')), parts along dimension 0
- gradient: float32 [32, 192, 128], P(('groups', 'slab'), 'shot'), parts along dimension 0
There are 2 independent parts, one for each index of `groups`. A program takes and returns all parts, laid end to end along the dimension named above; an argument that names none is the same for every part. Nothing has to cross between parts.
Inputs may be any that keep to these rules, and one draw needn't show every extreme that they name: `src_signs`: each entry is -1 or +1.
All inputs are finite; a program needn't handle non-finite values.
Results may differ from a plain program's by a relative error of at most 0.0001.
Values sent between devices are 32-bit elements; how exact they have to be, the bound alone decides.
No kernel may reach another device: no remote copies, remote signals or barrier semaphores. Data moves between devices by JAX's collectives and lax.ppermute only.
A program may use at most 64 MiB of HBM per device.

v0:
```python
import jax
import jax.numpy as jnp
from jax import lax
from jax.sharding import PartitionSpec as P

STEPS = 4
center_coef = -2.5
near_coef = 4.0 / 3.0
far_coef = -1.0 / 12.0
courant = 0.14
relax_decay = (0.3, 0.7, 0.95)
relax_weight = (0.3, 0.2, 0.1)
update_rate = 0.05
tiny_eps = 1e-06


def padded_2(block, sides, width):
    for axis, dim in sides:
        count = lax.axis_size(axis)
        forward = [(i, i + 1) for i in range(count - 1)]
        backward = [(target, source) for source, target in forward]
        low = lax.ppermute(
            lax.slice_in_dim(block, block.shape[dim] - width, None, axis=dim), axis, forward
        )
        high = lax.ppermute(lax.slice_in_dim(block, 0, width, axis=dim), axis, backward)
        block = jnp.concatenate([low, block, high], axis=dim)
    return block


def laplace(padded):
    middle = padded[2:-2]
    flanks = jnp.pad(middle, ((0, 0), (2, 2), (2, 2)))
    depth_sum = near_coef * (padded[3:-1] + padded[1:-3]) + far_coef * (padded[4:] + padded[:-4])
    cross_sum = near_coef * (flanks[:, 3:-1, 2:-2] + flanks[:, 1:-3, 2:-2]) + far_coef * (
        flanks[:, 4:, 2:-2] + flanks[:, :-4, 2:-2]
    )
    along_sum = near_coef * (flanks[:, 2:-2, 3:-1] + flanks[:, 2:-2, 1:-3]) + far_coef * (
        flanks[:, 2:-2, 4:] + flanks[:, 2:-2, :-4]
    )
    return 3.0 * center_coef * middle + depth_sum + cross_sum + along_sum


def place_sources(cells, signs, start, count):
    local = cells - start
    inside = (local >= 0) & (local < count)
    slot = jnp.where(inside, local, count)
    return jnp.zeros((count,), jnp.float32).at[slot].add(signs.astype(jnp.float32), mode="drop")


def per_device(
    slowness,
    wave_prev,
    wave_now,
    memory,
    adjoint_now,
    adjoint_prev,
    wavelet,
    src_cells,
    src_signs,
    rec_cells,
    observed,
):
    depth, width, lanes = slowness.shape
    plane = width * lanes
    block = depth * plane
    offset = lax.axis_index("slab") * block
    decay = jnp.array(relax_decay, jnp.float32)[:, None, None, None]
    weight = jnp.array(relax_weight, jnp.float32)[:, None, None, None]
    rec_local = rec_cells - offset
    rec_inside = (rec_local >= 0) & (rec_local < block)
    rec_slot = jnp.where(rec_inside, rec_local, block)
    rec_safe = jnp.minimum(rec_slot, block - 1)
    scaled = courant / (slowness * slowness)
    older, current, relax = (wave_prev[0], wave_now[0], memory[0])
    saved = []
    misfits = []

    def record(field, level):
        picked = field.reshape(-1)[rec_safe]
        misfits.append(jnp.where(rec_inside, picked - observed[0, level], 0.0))

    src_field = place_sources(src_cells[0], src_signs[0], offset, block).reshape(
        depth, width, lanes
    )
    for level in range(STEPS):
        padded = padded_2(current, (("slab", 0),), 2)
        curved = laplace(padded)
        accel = curved + jnp.sum(relax, 0)
        newer = 2.0 * current - older + scaled * accel + wavelet[level] * src_field
        relax = decay * relax - weight * curved[None]
        older, current = (current, newer)
        saved.append(accel)
        record(current, level)
    back_prev, back_now = (adjoint_prev[0], adjoint_now[0])
    back_relax = jnp.zeros_like(relax)
    accum = jnp.zeros_like(slowness)
    for level in reversed(range(STEPS)):
        inject = (
            jnp.zeros((block,), jnp.float32)
            .at[rec_slot]
            .add(misfits[level], mode="drop")
            .reshape(depth, width, lanes)
        )
        united = back_now + inject
        pushed = scaled * united
        drive = pushed - jnp.sum(weight * back_relax, 0)
        padded = padded_2(drive, (("slab", 0),), 2)
        accum = accum + united * saved[level]
        back_prev, back_now = (-united, back_prev + 2.0 * united + laplace(padded))
        back_relax = decay * back_relax + pushed[None]
    local_grad = accum * (-2.0 * courant / (slowness * slowness * slowness))
    cells_all = lax.axis_size("slab") * block
    share = width // lax.axis_size("shot")
    first = lax.axis_index("shot") * share
    summed = lax.psum(local_grad, "shot")
    squares = lax.psum(jnp.sum(summed * summed), "slab")
    rms_value = jnp.sqrt(squares / cells_all + tiny_eps)
    normed = summed / rms_value
    new_slowness = slowness - update_rate * normed
    gradient = lax.dynamic_slice_in_dim(normed, first, share, 1)
    return (new_slowness, gradient)


def solution(mesh):
    in_specs = (
        P(("groups", "slab"), None, None),
        P(("groups", "shot"), "slab", None, None),
        P(("groups", "shot"), "slab", None, None),
        P(("groups", "shot"), None, "slab", None, None),
        P(("groups", "shot"), "slab", None, None),
        P(("groups", "shot"), "slab", None, None),
        P(),
        P(("groups", "shot"), None),
        P(("groups", "shot"), None),
        P("groups"),
        P(("groups", "shot"), None, None),
    )
    out_specs = (P(("groups", "slab"), None, None), P(("groups", "slab"), "shot", None))
    return jax.shard_map(
        per_device, mesh=mesh, in_specs=in_specs, out_specs=out_specs, check_vma=False
    )
```

profile of v0, /device:TPU:0, one launch (start us, length us, event | category | flops | bytes accessed | tf_op | source)
XLA Modules:
  0.0 167.0 jit_solution(11458838551574252018)
XLA Ops:
  9.6 5.6 %collective-permute-start.1 = (f32[2,192,128]{2,1,0:T(8,128)S(1)}, f32[2,192,128]{2,1,0:T(8,128)S(1)}, u32[]{:S(2)}, u32[]{:S(2)}) collective-permute-start(f32[2,192,128]{2,1,0:T(8,128)S(1)} %get-tuple-element.43), channel_id=1, source_target_pairs={{0,1},{1,2},{2,3},{4,5},{5,6},{6,7},{8,9},{9,10},{10,11},{12,13},{... | collective-permute-start | bytes 589832 | tf_op jit(solution)/shard_map/ppermute | solution.py:22
  20.4 2.6 %broadcast_multiply_fusion.1 = (f32[98304]{0:T(1024)S(1)}, f32[98304]{0:T(1024)S(1)}, f32[98304]{0:T(1024)S(1)}, f32[98304]{0:T(1024)S(1)}) fusion(f32[98304]{0:T(1024)S(1)} %scatter_custom_fusion, f32[]{:T(128)} %bitcast.13, f32[]{:T(128)} %bitcast.15, f32[]{:T(128)} %bitcast.11, f32[]{:T(128)} %bitcast.5), kind=kLoop, calls=%fused_computation.281 | loop fusion | flops 393216 | bytes 1966096 | tf_op jit(solution)/shard_map/mul | solution.py:89
  25.8 4.6 %collective-permute-start.3 = (f32[2,192,128]{2,1,0:T(8,128)S(1)}, f32[2,192,128]{2,1,0:T(8,128)S(1)}, u32[]{:S(2)}, u32[]{:S(2)}) collective-permute-start(f32[2,192,128]{2,1,0:T(8,128)S(1)} %get-tuple-element.41), channel_id=1, source_target_pairs={{0,1},{1,2},{2,3},{4,5},{5,6},{6,7},{8,9},{9,10},{10,11},{12,13},{... | collective-permute-start | bytes 589832 | tf_op jit(solution)/shard_map/ppermute | solution.py:22
  30.6 2.1 %collective-permute-done.2 = f32[2,192,128]{2,1,0:T(8,128)S(1)} collective-permute-done((f32[2,192,128]{2,1,0:T(8,128)S(1)}, f32[2,192,128]{2,1,0:T(8,128)S(1)}, u32[]{:S(2)}, u32[]{:S(2)}) %collective-permute-start.2) | collective-permute-done | bytes 196640 | tf_op jit(solution)/shard_map/ppermute | solution.py:25
  35.8 5.0 %collective-permute-start.5 = (f32[2,192,128]{2,1,0:T(8,128)S(1)}, f32[2,192,128]{2,1,0:T(8,128)S(1)}, u32[]{:S(2)}, u32[]{:S(2)}) collective-permute-start(f32[2,192,128]{2,1,0:T(8,128)S(1)} %get-tuple-element.35), channel_id=1, source_target_pairs={{0,1},{1,2},{2,3},{4,5},{5,6},{6,7},{8,9},{9,10},{10,11},{12,13},{... | collective-permute-start | bytes 589832 | tf_op jit(solution)/shard_map/ppermute | solution.py:22
  47.2 5.0 %collective-permute-start.7 = (f32[2,192,128]{2,1,0:T(8,128)}, f32[2,192,128]{2,1,0:T(8,128)S(1)}, u32[]{:S(2)}, u32[]{:S(2)}) collective-permute-start(f32[2,192,128]{2,1,0:T(8,128)} %get-tuple-element.33), channel_id=1, source_target_pairs={{0,1},{1,2},{2,3},{4,5},{5,6},{6,7},{8,9},{9,10},{10,11},{12,13},{... | collective-permute-start | bytes 589832 | tf_op jit(solution)/shard_map/ppermute | solution.py:22
  52.8 2.3 %gather_fusion.3 = f32[256]{0:T(256)} fusion(f32[98304]{0:T(1024)S(1)} %bitcast.58, s32[1024]{0:T(1024)S(1)} %pad_clamp_fusion), kind=kCustom, calls=%fused_computation.3 | custom fusion | bytes 3072 | tf_op jit(solution)/shard_map/gather | solution.py:79
  55.2 2.3 %gather_fusion.2 = f32[256]{0:T(256)} fusion(f32[98304]{0:T(1024)S(1)} %bitcast.57, s32[1024]{0:T(1024)S(1)} %pad_clamp_fusion), kind=kCustom, calls=%fused_computation.2 | custom fusion | bytes 3072 | tf_op jit(solution)/shard_map/gather | solution.py:79
  57.5 2.3 %gather_fusion.1 = f32[256]{0:T(256)} fusion(f32[98304]{0:T(1024)S(1)} %bitcast.59, s32[1024]{0:T(1024)S(1)} %pad_clamp_fusion), kind=kCustom, calls=%fused_computation.1 | custom fusion | bytes 3072 | tf_op jit(solution)/shard_map/gather | solution.py:79
  60.5 1.6 add_add_fusion
  62.2 1.7 %gather_fusion = f32[256]{0:T(256)S(1)} fusion(f32[98304]{0:T(1024)S(1)} %bitcast.61, s32[1024]{0:T(1024)S(1)} %pad_clamp_fusion), kind=kCustom, calls=%fused_computation | custom fusion | bytes 3072 | tf_op jit(solution)/shard_map/gather | solution.py:79
  65.2 2.2 %scatter_custom_fusion.1 = f32[98304]{0:T(1024)S(1)} fusion(s32[256]{0:T(256)} %compare_select_fusion.1, f32[256]{0:T(256)S(1)} %get-tuple-element.51, f32[]{:T(128)} %constant.19.clone.1), kind=kCustom, calls=%fused_computation.292 | custom fusion | flops 256 | bytes 393728 | tf_op jit(solution)/shard_map/scatter-add | solution.py:101
  69.6 4.6 %collective-permute-start.9 = (f32[2,192,128]{2,1,0:T(8,128)}, f32[2,192,128]{2,1,0:T(8,128)S(1)}, u32[]{:S(2)}, u32[]{:S(2)}) collective-permute-start(f32[2,192,128]{2,1,0:T(8,128)} %get-tuple-element.31), channel_id=1, source_target_pairs={{0,1},{1,2},{2,3},{4,5},{5,6},{6,7},{8,9},{9,10},{10,11},{12,13},{... | collective-permute-start | bytes 589832 | tf_op jit(solution)/shard_map/ppermute | solution.py:22
  74.1 2.2 %scatter_custom_fusion.2 = f32[98304]{0:T(1024)S(1)} fusion(s32[256]{0:T(256)} %compare_select_fusion.1, f32[256]{0:T(256)} %get-tuple-element.50, f32[]{:T(128)} %constant.19.clone.1), kind=kCustom, calls=%fused_computation.290 | custom fusion | flops 256 | bytes 393728 | tf_op jit(solution)/shard_map/scatter-add | solution.py:101
  82.4 4.9 %collective-permute-start.11 = (f32[2,192,128]{2,1,0:T(8,128)S(1)}, f32[2,192,128]{2,1,0:T(8,128)S(1)}, u32[]{:S(2)}, u32[]{:S(2)}) collective-permute-start(f32[2,192,128]{2,1,0:T(8,128)S(1)} %get-tuple-element.29), channel_id=1, source_target_pairs={{0,1},{1,2},{2,3},{4,5},{5,6},{6,7},{8,9},{9,10},{10,11},{12,13},{... | collective-permute-start | bytes 589832 | tf_op jit(solution)/shard_map/ppermute | solution.py:22
  87.3 2.8 %scatter_custom_fusion.3 = f32[98304]{0:T(1024)} fusion(s32[256]{0:T(256)} %compare_select_fusion.1, f32[256]{0:T(256)} %get-tuple-element.48, f32[]{:T(128)} %constant.19.clone.1), kind=kCustom, calls=%fused_computation.288 | custom fusion | flops 256 | bytes 393728 | tf_op jit(solution)/shard_map/scatter-add | solution.py:101
  91.2 1.8 %multiply_subtract_fusion.2 = (f32[4,192,128]{2,1,0:T(8,128)S(1)}, f32[4,192,128]{2,1,0:T(8,128)S(1)}) fusion(f32[4,192,128]{2,1,0:T(8,128)} %get-tuple-element.5, f32[4,192,128]{2,1,0:T(8,128)S(1)} %copy-done, f32[4,192,128]{2,1,0:T(8,128)} %bitcast.66, f32[4,192,128]{2,1,0:T(8,128)S(1)} %fusion.169, f32[2,192,128]{2,1,0:T(8,128)} %copy-done.10, ...), kind=kLoop, calls=%fused_computation.275 | loop fusion | flops 3145728 | bytes 3538944 | tf_op jit(solution)/shard_map/sub | solution.py:106
  95.1 5.7 %collective-permute-start.13 = (f32[2,192,128]{2,1,0:T(8,128)}, f32[2,192,128]{2,1,0:T(8,128)}, u32[]{:S(2)}, u32[]{:S(2)}) collective-permute-start(f32[2,192,128]{2,1,0:T(8,128)} %get-tuple-element.27), channel_id=1, source_target_pairs={{0,1},{1,2},{2,3},{4,5},{5,6},{6,7},{8,9},{9,10},{10,11},{12,13},{... | collective-permute-start | bytes 589832 | tf_op jit(solution)/shard_map/ppermute | solution.py:22
  100.8 2.2 %scatter_custom_fusion.4 = f32[98304]{0:T(1024)S(1)} fusion(s32[256]{0:T(256)} %compare_select_fusion.1, f32[256]{0:T(256)S(1)} %get-tuple-element.49, f32[]{:T(128)} %constant.19.clone.1), kind=kCustom, calls=%fused_computation.286 | custom fusion | flops 256 | bytes 393728 | tf_op jit(solution)/shard_map/scatter-add | solution.py:101
  103.6 2.6 %fusion.4 = f32[4,192,128]{2,1,0:T(8,128)} fusion(f32[4,192,128]{2,1,0:T(8,128)S(1)} %copy-done, f32[4,192,128]{2,1,0:T(8,128)} %get-tuple-element.24, f32[4,192,128]{2,1,0:T(8,128)S(1)} %bitcast.65, f32[2,192,128]{2,1,0:T(8,128)} %collective-permute-done.13, f32[4,192,128]{2,1,0:T(8,128)S(1)} %get-tuple-element.8, ...), kind=kLoop, calls=%fused_computation.104 | loop fusion | flops 3833856 | bytes 4718592 | tf_op jit(solution)/shard_map/mul | solution.py:111
  106.2 36.8 %all-reduce.9.cloned.1.call-done = f32[4,192,128]{2,1,0:T(8,128)} async-done(((f32[4,192,128]{2,1,0:T(8,128)}), f32[4,192,128]{2,1,0:T(8,128)}) %all-reduce.9.cloned.1.call-update) | async-done | bytes 393232 | tf_op jit(solution)/shard_map/psum | solution.py:115
  143.0 1.7 %multiply_reduce_fusion.2 = f32[]{:T(128)} fusion(f32[4,192,128]{2,1,0:T(8,128)} %all-reduce.9.cloned.1.call-done), kind=kLoop, calls=%fused_computation.274 | loop fusion | flops 196607 | bytes 393220 | tf_op jit(solution)/shard_map/reduce_sum | solution.py:116
  144.7 12.3 %psum.15 = f32[]{:T(128)} all-reduce(f32[]{:T(128)} %multiply_reduce_fusion.2), channel_id=1, replica_groups=mesh['groups'=2,'shot'=4,'slab'=4] {'slab'}, use_global_device_ids=true, to_apply=%region_14.15 | all-reduce | flops 1 | bytes 8 | tf_op jit(solution)/shard_map/psum | solution.py:116
  157.7 1.8 %multiply_subtract_fusion.1 = (f32[4,192,128]{2,1,0:T(8,128)}, f32[4,192,128]{2,1,0:T(8,128)S(1)}) fusion(f32[4,192,128]{2,1,0:T(8,128)S(1)} %copy-done, f32[4,192,128]{2,1,0:T(8,128)} %all-reduce.9.cloned.1.call-done, f32[]{:T(128)S(6)} %sqrt.3), kind=kLoop, calls=%fused_computation.273 | loop fusion | flops 294912 | bytes 1572868 | tf_op jit(solution)/shard_map/sub | solution.py:119
  (84 shorter events, 35.0 us)
Async XLA Ops:
  7.2 135.9 %all-reduce.9.cloned.1.call-start = ((), (), s32[]{:S(2)}) async-start(), calls=%async_computation | async-start | bytes 786432 | tf_op jit(solution)/shard_map/psum | solution.py:115
  8.3 14.8 %collective-permute-start = (f32[2,192,128]{2,1,0:T(8,128)S(1)}, f32[2,192,128]{2,1,0:T(8,128)S(1)}, u32[]{:S(2)}, u32[]{:S(2)}) collective-permute-start(f32[2,192,128]{2,1,0:T(8,128)S(1)} %get-tuple-element.42), channel_id=1, source_target_pairs={{1,0},{2,1},{3,2},{5,4},{6,5},{7,6},{9,8},{10,9},{11,10},{13,12},{... | collective-permute-start | bytes 589832 | tf_op jit(solution)/shard_map/ppermute | solution.py:25
  9.6 13.5 %collective-permute-start.1 = (f32[2,192,128]{2,1,0:T(8,128)S(1)}, f32[2,192,128]{2,1,0:T(8,128)S(1)}, u32[]{:S(2)}, u32[]{:S(2)}) collective-permute-start(f32[2,192,128]{2,1,0:T(8,128)S(1)} %get-tuple-element.43), channel_id=1, source_target_pairs={{0,1},{1,2},{2,3},{4,5},{5,6},{6,7},{8,9},{9,10},{10,11},{12,13},{... | collective-permute-start | bytes 589832 | tf_op jit(solution)/shard_map/ppermute | solution.py:22
  19.3 3.8 %copy-start = (f32[4,192,128]{2,1,0:T(8,128)S(1)}, f32[4,192,128]{2,1,0:T(8,128)}, u32[]{:S(2)}) copy-start(f32[4,192,128]{2,1,0:T(8,128)} %param.13) | copy-start | bytes 1179652
  19.4 3.8 %copy-start.2 = (f32[1,4,192,128]{3,2,1,0:T(8,128)S(1)}, f32[1,4,192,128]{3,2,1,0:T(8,128)}, u32[]{:S(2)}) copy-start(f32[1,4,192,128]{3,2,1,0:T(8,128)} %param.15) | copy-start | bytes 1179652
  23.1 7.2 %copy-start.1 = (f32[1,3,4,192,128]{4,3,2,1,0:T(8,128)S(1)}, f32[1,3,4,192,128]{4,3,2,1,0:T(8,128)}, u32[]{:S(2)}) copy-start(f32[1,3,4,192,128]{4,3,2,1,0:T(8,128)} %param.16) | copy-start | bytes 3538948
  23.1 7.2 %copy-start.12 = (f32[3]{0:T(128)S(1)}, f32[3]{0:T(128)}, u32[]{:S(2)}) copy-start(f32[3]{0:T(128)} %constant.18.clone) | copy-start | bytes 40
  23.2 7.2 %copy-start.13 = (f32[3]{0:T(128)S(1)}, f32[3]{0:T(128)}, u32[]{:S(2)}) copy-start(f32[3]{0:T(128)} %constant.50.clone) | copy-start | bytes 40
  24.5 8.3 %collective-permute-start.2 = (f32[2,192,128]{2,1,0:T(8,128)S(1)}, f32[2,192,128]{2,1,0:T(8,128)S(1)}, u32[]{:S(2)}, u32[]{:S(2)}) collective-permute-start(f32[2,192,128]{2,1,0:T(8,128)S(1)} %get-tuple-element.40), channel_id=1, source_target_pairs={{1,0},{2,1},{3,2},{5,4},{6,5},{7,6},{9,8},{10,9},{11,10},{13,12},{... | collective-permute-start | bytes 589832 | tf_op jit(solution)/shard_map/ppermute | solution.py:25
  25.8 8.1 %collective-permute-start.3 = (f32[2,192,128]{2,1,0:T(8,128)S(1)}, f32[2,192,128]{2,1,0:T(8,128)S(1)}, u32[]{:S(2)}, u32[]{:S(2)}) collective-permute-start(f32[2,192,128]{2,1,0:T(8,128)S(1)} %get-tuple-element.41), channel_id=1, source_target_pairs={{0,1},{1,2},{2,3},{4,5},{5,6},{6,7},{8,9},{9,10},{10,11},{12,13},{... | collective-permute-start | bytes 589832 | tf_op jit(solution)/shard_map/ppermute | solution.py:22
  33.9 6.9 %copy-start.16 = (f32[1,4,256]{2,1,0:T(4,128)S(1)}, f32[1,4,256]{2,1,0:T(4,128)}, u32[]{:S(2)}) copy-start(f32[1,4,256]{2,1,0:T(4,128)} %param.23) | copy-start | bytes 12292
  34.5 8.0 %collective-permute-start.4 = (f32[2,192,128]{2,1,0:T(8,128)S(1)}, f32[2,192,128]{2,1,0:T(8,128)S(1)}, u32[]{:S(2)}, u32[]{:S(2)}) collective-permute-start(f32[2,192,128]{2,1,0:T(8,128)S(1)} %get-tuple-element.34), channel_id=1, source_target_pairs={{1,0},{2,1},{3,2},{5,4},{6,5},{7,6},{9,8},{10,9},{11,10},{13,12},{... | collective-permute-start | bytes 589832 | tf_op jit(solution)/shard_map/ppermute | solution.py:25
  35.8 8.2 %collective-permute-start.5 = (f32[2,192,128]{2,1,0:T(8,128)S(1)}, f32[2,192,128]{2,1,0:T(8,128)S(1)}, u32[]{:S(2)}, u32[]{:S(2)}) collective-permute-start(f32[2,192,128]{2,1,0:T(8,128)S(1)} %get-tuple-element.35), channel_id=1, source_target_pairs={{0,1},{1,2},{2,3},{4,5},{5,6},{6,7},{8,9},{9,10},{10,11},{12,13},{... | collective-permute-start | bytes 589832 | tf_op jit(solution)/shard_map/ppermute | solution.py:22
  45.0 7.3 %copy-start.15 = (s32[256]{0:T(256)S(1)}, s32[256]{0:T(256)}, u32[]{:S(2)}) copy-start(s32[256]{0:T(256)} %param.22) | copy-start | bytes 3076
  45.9 13.8 %collective-permute-start.6 = (f32[2,192,128]{2,1,0:T(8,128)}, f32[2,192,128]{2,1,0:T(8,128)S(1)}, u32[]{:S(2)}, u32[]{:S(2)}) collective-permute-start(f32[2,192,128]{2,1,0:T(8,128)} %get-tuple-element.32), channel_id=1, source_target_pairs={{1,0},{2,1},{3,2},{5,4},{6,5},{7,6},{9,8},{10,9},{11,10},{13,12},{... | collective-permute-start | bytes 589832 | tf_op jit(solution)/shard_map/ppermute | solution.py:25
  47.2 12.5 %collective-permute-start.7 = (f32[2,192,128]{2,1,0:T(8,128)}, f32[2,192,128]{2,1,0:T(8,128)S(1)}, u32[]{:S(2)}, u32[]{:S(2)}) collective-permute-start(f32[2,192,128]{2,1,0:T(8,128)} %get-tuple-element.33), channel_id=1, source_target_pairs={{0,1},{1,2},{2,3},{4,5},{5,6},{6,7},{8,9},{9,10},{10,11},{12,13},{... | collective-permute-start | bytes 589832 | tf_op jit(solution)/shard_map/ppermute | solution.py:22
  62.2 5.2 %copy-start.4 = (f32[1,4,192,128]{3,2,1,0:T(8,128)S(1)}, f32[1,4,192,128]{3,2,1,0:T(8,128)}, u32[]{:S(2)}) copy-start(f32[1,4,192,128]{3,2,1,0:T(8,128)} %param.17) | copy-start | bytes 1179652
  67.4 10.9 %copy-start.3 = (f32[1,4,192,128]{3,2,1,0:T(8,128)S(1)}, f32[1,4,192,128]{3,2,1,0:T(8,128)}, u32[]{:S(2)}) copy-start(f32[1,4,192,128]{3,2,1,0:T(8,128)} %param.18) | copy-start | bytes 1179652
  68.3 8.1 %collective-permute-start.8 = (f32[2,192,128]{2,1,0:T(8,128)}, f32[2,192,128]{2,1,0:T(8,128)S(1)}, u32[]{:S(2)}, u32[]{:S(2)}) collective-permute-start(f32[2,192,128]{2,1,0:T(8,128)} %get-tuple-element.30), channel_id=1, source_target_pairs={{1,0},{2,1},{3,2},{5,4},{6,5},{7,6},{9,8},{10,9},{11,10},{13,12},{... | collective-permute-start | bytes 589832 | tf_op jit(solution)/shard_map/ppermute | solution.py:25
  69.6 8.0 %collective-permute-start.9 = (f32[2,192,128]{2,1,0:T(8,128)}, f32[2,192,128]{2,1,0:T(8,128)S(1)}, u32[]{:S(2)}, u32[]{:S(2)}) collective-permute-start(f32[2,192,128]{2,1,0:T(8,128)} %get-tuple-element.31), channel_id=1, source_target_pairs={{0,1},{1,2},{2,3},{4,5},{5,6},{6,7},{8,9},{9,10},{10,11},{12,13},{... | collective-permute-start | bytes 589832 | tf_op jit(solution)/shard_map/ppermute | solution.py:22
  81.1 9.1 %collective-permute-start.10 = (f32[2,192,128]{2,1,0:T(8,128)S(1)}, f32[2,192,128]{2,1,0:T(8,128)S(1)}, u32[]{:S(2)}, u32[]{:S(2)}) collective-permute-start(f32[2,192,128]{2,1,0:T(8,128)S(1)} %get-tuple-element.28), channel_id=1, source_target_pairs={{1,0},{2,1},{3,2},{5,4},{6,5},{7,6},{9,8},{10,9},{11,10},{13,12},{... | collective-permute-start | bytes 589832 | tf_op jit(solution)/shard_map/ppermute | solution.py:25
  82.4 8.1 %collective-permute-start.11 = (f32[2,192,128]{2,1,0:T(8,128)S(1)}, f32[2,192,128]{2,1,0:T(8,128)S(1)}, u32[]{:S(2)}, u32[]{:S(2)}) collective-permute-start(f32[2,192,128]{2,1,0:T(8,128)S(1)} %get-tuple-element.29), channel_id=1, source_target_pairs={{0,1},{1,2},{2,3},{4,5},{5,6},{6,7},{8,9},{9,10},{10,11},{12,13},{... | collective-permute-start | bytes 589832 | tf_op jit(solution)/shard_map/ppermute | solution.py:22
  93.8 9.2 %collective-permute-start.12 = (f32[2,192,128]{2,1,0:T(8,128)}, f32[2,192,128]{2,1,0:T(8,128)}, u32[]{:S(2)}, u32[]{:S(2)}) collective-permute-start(f32[2,192,128]{2,1,0:T(8,128)} %get-tuple-element.26), channel_id=1, source_target_pairs={{1,0},{2,1},{3,2},{5,4},{6,5},{7,6},{9,8},{10,9},{11,10},{13,12},{... | collective-permute-start | bytes 589832 | tf_op jit(solution)/shard_map/ppermute | solution.py:25
  95.1 8.5 %collective-permute-start.13 = (f32[2,192,128]{2,1,0:T(8,128)}, f32[2,192,128]{2,1,0:T(8,128)}, u32[]{:S(2)}, u32[]{:S(2)}) collective-permute-start(f32[2,192,128]{2,1,0:T(8,128)} %get-tuple-element.27), channel_id=1, source_target_pairs={{0,1},{1,2},{2,3},{4,5},{5,6},{6,7},{8,9},{9,10},{10,11},{12,13},{... | collective-permute-start | bytes 589832 | tf_op jit(solution)/shard_map/ppermute | solution.py:22
  (8 other events, 12.2 us)
Sparse Core Ops, SparseCore 0:
  106.3 36.6 all-reduce.8
where the time goes:
time: 168 us; the launch traced here: 167 us
  waiting for transfers between devices  44.9 us (27%)
  starting transfers between devices  44.4 us (26%)
  other arithmetic  33.3 us (20%)
  local copies, waits for them, and re-layouts  17 us (10%)
  between operations  15.2 us (9%)
  blocking collectives  12.3 us (7%)
    psum x1, waiting for transfers between devices, per_device(): summed = lax.psum(local_grad, 'shot')  36.8 us
    ppermute x7, starting transfers between devices, padded_2(): lax.ppermute(lax.slice_in_dim(block, block.shape[dim] - width, None, axis...  35.4 us
    psum x1, blocking collectives, per_device(): squares = lax.psum(jnp.sum(summed * summed), 'slab')  12.3 us
    scatter-add x4, other arithmetic, per_device(): inject = jnp.zeros((block,), jnp.float32).at[rec_slot].add(misfits[level]...  9.37 us
    ppermute x7, starting transfers between devices, padded_2(): lax.ppermute(lax.slice_in_dim(block, 0, width, axis=dim), axis, backward)  9.01 us
    gather x4, local copies, waits for them, and re-layouts, record(): picked = field.reshape(-1)[rec_safe]  8.65 us
    ppermute x7, waiting for transfers between devices, padded_2(): lax.ppermute(lax.slice_in_dim(block, block.shape[dim] - width, None, axis...  4.85 us
    add x4, other arithmetic, per_device(): newer = 2.0 * current - older + scaled * accel + wavelet[level] * src_field  3.63 us
  transfers between devices with their start and end apart: 15, of which 8 were waited for; matrix products, arithmetic and copies ran while one was open for 14% of the time, Pallas kernels for 0%

commit v1 on v0

--- a/solution.py
+++ b/solution.py
@@ -112,7 +112,8 @@
     cells_all = lax.axis_size("slab") * block
     share = width // lax.axis_size("shot")
     first = lax.axis_index("shot") * share
-    summed = lax.psum(local_grad, "shot")
+    parts = lax.all_gather(local_grad, "shot")
+    summed = jnp.sum(parts, axis=0)
     squares = lax.psum(jnp.sum(summed * summed), "slab")
     rms_value = jnp.sqrt(squares / cells_all + tiny_eps)
     normed = summed / rms_value

time: 168 us -> 154 us (0.917)
  waiting for transfers between devices: 44.9 us -> 31.7 us
    psum x1 -> x0, waiting for transfers between devices: 36.8 us -> none  [per_device(): summed = lax.psum(local_grad, 'shot')]
    all_gather x0 -> x1, waiting for transfers between devices: none -> 23.7 us  [per_device(): parts = lax.all_gather(local_grad, 'shot')]
  transfers between devices with their start and end apart: 15 -> 15, of which waited for: 8 -> 8; matrix products, arithmetic and copies ran while one was open for 14% -> 15% of each run, Pallas kernels for 0% -> 0%
where the time goes in v1:
time: 154 us; the launch traced here: 153 us
  starting transfers between devices  44.4 us (29%)
  other arithmetic  32.8 us (21%)
  waiting for transfers between devices  31.7 us (21%)
  local copies, waits for them, and re-layouts  17 us (11%)
  between operations  15.2 us (10%)
  blocking collectives  12.3 us (8%)
    ppermute x7, starting transfers between devices, padded_2(): lax.ppermute(lax.slice_in_dim(block, block.shape[dim] - width, None, axis...  35.4 us
    all_gather x1, waiting for transfers between devices, per_device(): parts = lax.all_gather(local_grad, 'shot')  23.7 us
    psum x1, blocking collectives, per_device(): squares = lax.psum(jnp.sum(summed * summed), 'slab')  12.3 us
    scatter-add x4, other arithmetic, per_device(): inject = jnp.zeros((block,), jnp.float32).at[rec_slot].add(misfits[level]...  9.37 us
    ppermute x7, starting transfers between devices, padded_2(): lax.ppermute(lax.slice_in_dim(block, 0, width, axis=dim), axis, backward)  9.01 us
    gather x4, local copies, waits for them, and re-layouts, record(): picked = field.reshape(-1)[rec_safe]  8.65 us
    ppermute x7, waiting for transfers between devices, padded_2(): lax.ppermute(lax.slice_in_dim(block, block.shape[dim] - width, None, axis...  4.85 us
    add x4, other arithmetic, per_device(): newer = 2.0 * current - older + scaled * accel + wavelet[level] * src_field  3.63 us
  transfers between devices with their start and end apart: 15, of which 8 were waited for; matrix products, arithmetic and copies ran while one was open for 15% of the time, Pallas kernels for 0%

profile of v1, /device:TPU:0, one launch (start us, length us, event | category | flops | bytes accessed | tf_op | source)
XLA Modules:
  0.0 153.4 jit_solution(5797508484560830545)
XLA Ops:
  9.6 5.6 %collective-permute-start.1 = (f32[2,192,128]{2,1,0:T(8,128)S(1)}, f32[2,192,128]{2,1,0:T(8,128)S(1)}, u32[]{:S(2)}, u32[]{:S(2)}) collective-permute-start(f32[2,192,128]{2,1,0:T(8,128)S(1)} %get-tuple-element.43), channel_id=1, source_target_pairs={{0,1},{1,2},{2,3},{4,5},{5,6},{6,7},{8,9},{9,10},{10,11},{12,13},{... | collective-permute-start | bytes 589832 | tf_op jit(solution)/shard_map/ppermute | solution.py:22
  20.4 2.6 %broadcast_multiply_fusion.1 = (f32[98304]{0:T(1024)S(1)}, f32[98304]{0:T(1024)S(1)}, f32[98304]{0:T(1024)S(1)}, f32[98304]{0:T(1024)S(1)}) fusion(f32[98304]{0:T(1024)S(1)} %scatter_custom_fusion, f32[]{:T(128)} %bitcast.13, f32[]{:T(128)} %bitcast.15, f32[]{:T(128)} %bitcast.11, f32[]{:T(128)} %bitcast.5), kind=kLoop, calls=%fused_computation.281 | loop fusion | flops 393216 | bytes 1966096 | tf_op jit(solution)/shard_map/mul | solution.py:89
  25.8 4.6 %collective-permute-start.3 = (f32[2,192,128]{2,1,0:T(8,128)S(1)}, f32[2,192,128]{2,1,0:T(8,128)S(1)}, u32[]{:S(2)}, u32[]{:S(2)}) collective-permute-start(f32[2,192,128]{2,1,0:T(8,128)S(1)} %get-tuple-element.41), channel_id=1, source_target_pairs={{0,1},{1,2},{2,3},{4,5},{5,6},{6,7},{8,9},{9,10},{10,11},{12,13},{... | collective-permute-start | bytes 589832 | tf_op jit(solution)/shard_map/ppermute | solution.py:22
  30.6 2.1 %collective-permute-done.2 = f32[2,192,128]{2,1,0:T(8,128)S(1)} collective-permute-done((f32[2,192,128]{2,1,0:T(8,128)S(1)}, f32[2,192,128]{2,1,0:T(8,128)S(1)}, u32[]{:S(2)}, u32[]{:S(2)}) %collective-permute-start.2) | collective-permute-done | bytes 196640 | tf_op jit(solution)/shard_map/ppermute | solution.py:25
  35.8 5.0 %collective-permute-start.5 = (f32[2,192,128]{2,1,0:T(8,128)S(1)}, f32[2,192,128]{2,1,0:T(8,128)S(1)}, u32[]{:S(2)}, u32[]{:S(2)}) collective-permute-start(f32[2,192,128]{2,1,0:T(8,128)S(1)} %get-tuple-element.35), channel_id=1, source_target_pairs={{0,1},{1,2},{2,3},{4,5},{5,6},{6,7},{8,9},{9,10},{10,11},{12,13},{... | collective-permute-start | bytes 589832 | tf_op jit(solution)/shard_map/ppermute | solution.py:22
  47.2 5.0 %collective-permute-start.7 = (f32[2,192,128]{2,1,0:T(8,128)}, f32[2,192,128]{2,1,0:T(8,128)S(1)}, u32[]{:S(2)}, u32[]{:S(2)}) collective-permute-start(f32[2,192,128]{2,1,0:T(8,128)} %get-tuple-element.33), channel_id=1, source_target_pairs={{0,1},{1,2},{2,3},{4,5},{5,6},{6,7},{8,9},{9,10},{10,11},{12,13},{... | collective-permute-start | bytes 589832 | tf_op jit(solution)/shard_map/ppermute | solution.py:22
  52.8 2.3 %gather_fusion.3 = f32[256]{0:T(256)} fusion(f32[98304]{0:T(1024)S(1)} %bitcast.59, s32[1024]{0:T(1024)S(1)} %pad_clamp_fusion), kind=kCustom, calls=%fused_computation.3 | custom fusion | bytes 3072 | tf_op jit(solution)/shard_map/gather | solution.py:79
  55.2 2.3 %gather_fusion.2 = f32[256]{0:T(256)} fusion(f32[98304]{0:T(1024)S(1)} %bitcast.58, s32[1024]{0:T(1024)S(1)} %pad_clamp_fusion), kind=kCustom, calls=%fused_computation.2 | custom fusion | bytes 3072 | tf_op jit(solution)/shard_map/gather | solution.py:79
  57.5 2.3 %gather_fusion.1 = f32[256]{0:T(256)} fusion(f32[98304]{0:T(1024)S(1)} %bitcast.60, s32[1024]{0:T(1024)S(1)} %pad_clamp_fusion), kind=kCustom, calls=%fused_computation.1 | custom fusion | bytes 3072 | tf_op jit(solution)/shard_map/gather | solution.py:79
  60.5 1.6 %add_add_fusion = (f32[4,192,128]{2,1,0:T(8,128)S(1)}, f32[4,192,128]{2,1,0:T(8,128)S(1)}) fusion(f32[4,192,128]{2,1,0:T(8,128)S(1)} %bitcast.63, f32[4,192,128]{2,1,0:T(8,128)S(1)} %get-tuple-element.18, f32[4,192,128]{2,1,0:T(8,128)S(1)} %get-tuple-element.16, f32[4,192,128]{2,1,0:T(8,128)S(1)} %copy-done, f32[4,192,128]{2,1,0:T(8,128)S(1)} %get-tuple-element.3, ...), kind=kLoop, calls=%fused_computation.276 | loop fusion | flops 3047424 | bytes 3145728 | tf_op jit(solution)/shard_map/add | solution.py:89
  62.2 1.7 %gather_fusion = f32[256]{0:T(256)S(1)} fusion(f32[98304]{0:T(1024)S(1)} %bitcast.62, s32[1024]{0:T(1024)S(1)} %pad_clamp_fusion), kind=kCustom, calls=%fused_computation | custom fusion | bytes 3072 | tf_op jit(solution)/shard_map/gather | solution.py:79
  65.2 2.2 %scatter_custom_fusion.1 = f32[98304]{0:T(1024)S(1)} fusion(s32[256]{0:T(256)} %compare_select_fusion.1, f32[256]{0:T(256)S(1)} %get-tuple-element.51, f32[]{:T(128)} %constant.19.clone.1), kind=kCustom, calls=%fused_computation.292 | custom fusion | flops 256 | bytes 393728 | tf_op jit(solution)/shard_map/scatter-add | solution.py:101
  69.6 4.6 %collective-permute-start.9 = (f32[2,192,128]{2,1,0:T(8,128)}, f32[2,192,128]{2,1,0:T(8,128)S(1)}, u32[]{:S(2)}, u32[]{:S(2)}) collective-permute-start(f32[2,192,128]{2,1,0:T(8,128)} %get-tuple-element.31), channel_id=1, source_target_pairs={{0,1},{1,2},{2,3},{4,5},{5,6},{6,7},{8,9},{9,10},{10,11},{12,13},{... | collective-permute-start | bytes 589832 | tf_op jit(solution)/shard_map/ppermute | solution.py:22
  74.1 2.2 %scatter_custom_fusion.2 = f32[98304]{0:T(1024)S(1)} fusion(s32[256]{0:T(256)} %compare_select_fusion.1, f32[256]{0:T(256)} %get-tuple-element.50, f32[]{:T(128)} %constant.19.clone.1), kind=kCustom, calls=%fused_computation.290 | custom fusion | flops 256 | bytes 393728 | tf_op jit(solution)/shard_map/scatter-add | solution.py:101
  78.3 1.6 %fusion.167 = (f32[4,192,128]{2,1,0:T(8,128)S(1)}, f32[4,192,128]{2,1,0:T(8,128)S(1)}) fusion(f32[4,192,128]{2,1,0:T(8,128)S(1)} %copy-done, f32[4,192,128]{2,1,0:T(8,128)S(1)} %bitcast.68, f32[4,192,128]{2,1,0:T(8,128)S(1)} %get-tuple-element.12, f32[2,192,128]{2,1,0:T(8,128)} %copy-done.11, f32[2,192,128]{2,1,0:T(8,128)} %copy-done.9, ...), kind=kLoop, calls=%fused_computation.310 | loop fusion | flops 2949120 | bytes 3145728 | tf_op jit(solution)/shard_map/mul | solution.py:105
  82.4 4.9 %collective-permute-start.11 = (f32[2,192,128]{2,1,0:T(8,128)S(1)}, f32[2,192,128]{2,1,0:T(8,128)S(1)}, u32[]{:S(2)}, u32[]{:S(2)}) collective-permute-start(f32[2,192,128]{2,1,0:T(8,128)S(1)} %get-tuple-element.29), channel_id=1, source_target_pairs={{0,1},{1,2},{2,3},{4,5},{5,6},{6,7},{8,9},{9,10},{10,11},{12,13},{... | collective-permute-start | bytes 589832 | tf_op jit(solution)/shard_map/ppermute | solution.py:22
  87.3 2.8 %scatter_custom_fusion.3 = f32[98304]{0:T(1024)} fusion(s32[256]{0:T(256)} %compare_select_fusion.1, f32[256]{0:T(256)} %get-tuple-element.48, f32[]{:T(128)} %constant.19.clone.1), kind=kCustom, calls=%fused_computation.288 | custom fusion | flops 256 | bytes 393728 | tf_op jit(solution)/shard_map/scatter-add | solution.py:101
  91.2 1.8 %multiply_subtract_fusion.2 = (f32[4,192,128]{2,1,0:T(8,128)S(1)}, f32[4,192,128]{2,1,0:T(8,128)S(1)}) fusion(f32[4,192,128]{2,1,0:T(8,128)} %get-tuple-element.5, f32[4,192,128]{2,1,0:T(8,128)S(1)} %copy-done, f32[4,192,128]{2,1,0:T(8,128)} %bitcast.67, f32[4,192,128]{2,1,0:T(8,128)S(1)} %fusion.169, f32[2,192,128]{2,1,0:T(8,128)} %copy-done.10, ...), kind=kLoop, calls=%fused_computation.275 | loop fusion | flops 3145728 | bytes 3538944 | tf_op jit(solution)/shard_map/sub | solution.py:106
  95.1 5.7 %collective-permute-start.13 = (f32[2,192,128]{2,1,0:T(8,128)}, f32[2,192,128]{2,1,0:T(8,128)}, u32[]{:S(2)}, u32[]{:S(2)}) collective-permute-start(f32[2,192,128]{2,1,0:T(8,128)} %get-tuple-element.27), channel_id=1, source_target_pairs={{0,1},{1,2},{2,3},{4,5},{5,6},{6,7},{8,9},{9,10},{10,11},{12,13},{... | collective-permute-start | bytes 589832 | tf_op jit(solution)/shard_map/ppermute | solution.py:22
  100.8 2.2 %scatter_custom_fusion.4 = f32[98304]{0:T(1024)S(1)} fusion(s32[256]{0:T(256)} %compare_select_fusion.1, f32[256]{0:T(256)S(1)} %get-tuple-element.49, f32[]{:T(128)} %constant.19.clone.1), kind=kCustom, calls=%fused_computation.286 | custom fusion | flops 256 | bytes 393728 | tf_op jit(solution)/shard_map/scatter-add | solution.py:101
  103.6 2.6 %fusion.4 = f32[4,192,128]{2,1,0:T(8,128)} fusion(f32[4,192,128]{2,1,0:T(8,128)S(1)} %copy-done, f32[4,192,128]{2,1,0:T(8,128)} %get-tuple-element.24, f32[4,192,128]{2,1,0:T(8,128)S(1)} %bitcast.66, f32[2,192,128]{2,1,0:T(8,128)} %collective-permute-done.13, f32[4,192,128]{2,1,0:T(8,128)S(1)} %get-tuple-element.8, ...), kind=kLoop, calls=%fused_computation.104 | loop fusion | flops 3833856 | bytes 4718592 | tf_op jit(solution)/shard_map/mul | solution.py:111
  106.2 23.7 %all-gather.3.cloned.1.call-done = f32[16,192,128]{2,1,0:T(8,128)} async-done(((f32[4,192,128]{2,1,0:T(8,128)}), f32[16,192,128]{2,1,0:T(8,128)}) %all-gather.3.cloned.1.call-update) | async-done | bytes 1572880 | tf_op jit(solution)/shard_map/all_gather | solution.py:115
  129.9 1.5 reduce_sum.91
  132.1 12.3 %psum.7 = f32[]{:T(128)} all-reduce(f32[]{:T(128)} %multiply_reduce_fusion.2), channel_id=1, replica_groups=mesh['groups'=2,'shot'=4,'slab'=4] {'slab'}, use_global_device_ids=true, to_apply=%region_14.15 | all-reduce | flops 1 | bytes 8 | tf_op jit(solution)/shard_map/psum | solution.py:117
  (85 shorter events, 34.9 us)
Async XLA Ops:
  7.2 122.7 %all-gather.3.cloned.1.call-start = ((), (), s32[]{:S(2)}) async-start(), calls=%async_computation | async-start | bytes 1966080 | tf_op jit(solution)/shard_map/all_gather | solution.py:115
  8.3 14.8 %collective-permute-start = (f32[2,192,128]{2,1,0:T(8,128)S(1)}, f32[2,192,128]{2,1,0:T(8,128)S(1)}, u32[]{:S(2)}, u32[]{:S(2)}) collective-permute-start(f32[2,192,128]{2,1,0:T(8,128)S(1)} %get-tuple-element.42), channel_id=1, source_target_pairs={{1,0},{2,1},{3,2},{5,4},{6,5},{7,6},{9,8},{10,9},{11,10},{13,12},{... | collective-permute-start | bytes 589832 | tf_op jit(solution)/shard_map/ppermute | solution.py:25
  9.6 13.5 %collective-permute-start.1 = (f32[2,192,128]{2,1,0:T(8,128)S(1)}, f32[2,192,128]{2,1,0:T(8,128)S(1)}, u32[]{:S(2)}, u32[]{:S(2)}) collective-permute-start(f32[2,192,128]{2,1,0:T(8,128)S(1)} %get-tuple-element.43), channel_id=1, source_target_pairs={{0,1},{1,2},{2,3},{4,5},{5,6},{6,7},{8,9},{9,10},{10,11},{12,13},{... | collective-permute-start | bytes 589832 | tf_op jit(solution)/shard_map/ppermute | solution.py:22
  19.3 3.8 %copy-start = (f32[4,192,128]{2,1,0:T(8,128)S(1)}, f32[4,192,128]{2,1,0:T(8,128)}, u32[]{:S(2)}) copy-start(f32[4,192,128]{2,1,0:T(8,128)} %param.13) | copy-start | bytes 1179652
  19.4 3.8 %copy-start.2 = (f32[1,4,192,128]{3,2,1,0:T(8,128)S(1)}, f32[1,4,192,128]{3,2,1,0:T(8,128)}, u32[]{:S(2)}) copy-start(f32[1,4,192,128]{3,2,1,0:T(8,128)} %param.15) | copy-start | bytes 1179652
  23.1 7.2 %copy-start.1 = (f32[1,3,4,192,128]{4,3,2,1,0:T(8,128)S(1)}, f32[1,3,4,192,128]{4,3,2,1,0:T(8,128)}, u32[]{:S(2)}) copy-start(f32[1,3,4,192,128]{4,3,2,1,0:T(8,128)} %param.16) | copy-start | bytes 3538948
  23.1 7.2 %copy-start.12 = (f32[3]{0:T(128)S(1)}, f32[3]{0:T(128)}, u32[]{:S(2)}) copy-start(f32[3]{0:T(128)} %constant.18.clone) | copy-start | bytes 40
  23.2 7.2 %copy-start.13 = (f32[3]{0:T(128)S(1)}, f32[3]{0:T(128)}, u32[]{:S(2)}) copy-start(f32[3]{0:T(128)} %constant.50.clone) | copy-start | bytes 40
  24.5 8.3 %collective-permute-start.2 = (f32[2,192,128]{2,1,0:T(8,128)S(1)}, f32[2,192,128]{2,1,0:T(8,128)S(1)}, u32[]{:S(2)}, u32[]{:S(2)}) collective-permute-start(f32[2,192,128]{2,1,0:T(8,128)S(1)} %get-tuple-element.40), channel_id=1, source_target_pairs={{1,0},{2,1},{3,2},{5,4},{6,5},{7,6},{9,8},{10,9},{11,10},{13,12},{... | collective-permute-start | bytes 589832 | tf_op jit(solution)/shard_map/ppermute | solution.py:25
  25.8 8.1 %collective-permute-start.3 = (f32[2,192,128]{2,1,0:T(8,128)S(1)}, f32[2,192,128]{2,1,0:T(8,128)S(1)}, u32[]{:S(2)}, u32[]{:S(2)}) collective-permute-start(f32[2,192,128]{2,1,0:T(8,128)S(1)} %get-tuple-element.41), channel_id=1, source_target_pairs={{0,1},{1,2},{2,3},{4,5},{5,6},{6,7},{8,9},{9,10},{10,11},{12,13},{... | collective-permute-start | bytes 589832 | tf_op jit(solution)/shard_map/ppermute | solution.py:22
  33.9 6.9 %copy-start.16 = (f32[1,4,256]{2,1,0:T(4,128)S(1)}, f32[1,4,256]{2,1,0:T(4,128)}, u32[]{:S(2)}) copy-start(f32[1,4,256]{2,1,0:T(4,128)} %param.23) | copy-start | bytes 12292
  34.5 8.0 %collective-permute-start.4 = (f32[2,192,128]{2,1,0:T(8,128)S(1)}, f32[2,192,128]{2,1,0:T(8,128)S(1)}, u32[]{:S(2)}, u32[]{:S(2)}) collective-permute-start(f32[2,192,128]{2,1,0:T(8,128)S(1)} %get-tuple-element.34), channel_id=1, source_target_pairs={{1,0},{2,1},{3,2},{5,4},{6,5},{7,6},{9,8},{10,9},{11,10},{13,12},{... | collective-permute-start | bytes 589832 | tf_op jit(solution)/shard_map/ppermute | solution.py:25
  35.8 8.2 %collective-permute-start.5 = (f32[2,192,128]{2,1,0:T(8,128)S(1)}, f32[2,192,128]{2,1,0:T(8,128)S(1)}, u32[]{:S(2)}, u32[]{:S(2)}) collective-permute-start(f32[2,192,128]{2,1,0:T(8,128)S(1)} %get-tuple-element.35), channel_id=1, source_target_pairs={{0,1},{1,2},{2,3},{4,5},{5,6},{6,7},{8,9},{9,10},{10,11},{12,13},{... | collective-permute-start | bytes 589832 | tf_op jit(solution)/shard_map/ppermute | solution.py:22
  45.0 7.3 %copy-start.15 = (s32[256]{0:T(256)S(1)}, s32[256]{0:T(256)}, u32[]{:S(2)}) copy-start(s32[256]{0:T(256)} %param.22) | copy-start | bytes 3076
  45.9 13.8 %collective-permute-start.6 = (f32[2,192,128]{2,1,0:T(8,128)}, f32[2,192,128]{2,1,0:T(8,128)S(1)}, u32[]{:S(2)}, u32[]{:S(2)}) collective-permute-start(f32[2,192,128]{2,1,0:T(8,128)} %get-tuple-element.32), channel_id=1, source_target_pairs={{1,0},{2,1},{3,2},{5,4},{6,5},{7,6},{9,8},{10,9},{11,10},{13,12},{... | collective-permute-start | bytes 589832 | tf_op jit(solution)/shard_map/ppermute | solution.py:25
  47.2 12.5 %collective-permute-start.7 = (f32[2,192,128]{2,1,0:T(8,128)}, f32[2,192,128]{2,1,0:T(8,128)S(1)}, u32[]{:S(2)}, u32[]{:S(2)}) collective-permute-start(f32[2,192,128]{2,1,0:T(8,128)} %get-tuple-element.33), channel_id=1, source_target_pairs={{0,1},{1,2},{2,3},{4,5},{5,6},{6,7},{8,9},{9,10},{10,11},{12,13},{... | collective-permute-start | bytes 589832 | tf_op jit(solution)/shard_map/ppermute | solution.py:22
  62.2 5.2 %copy-start.4 = (f32[1,4,192,128]{3,2,1,0:T(8,128)S(1)}, f32[1,4,192,128]{3,2,1,0:T(8,128)}, u32[]{:S(2)}) copy-start(f32[1,4,192,128]{3,2,1,0:T(8,128)} %param.17) | copy-start | bytes 1179652
  67.4 10.9 %copy-start.3 = (f32[1,4,192,128]{3,2,1,0:T(8,128)S(1)}, f32[1,4,192,128]{3,2,1,0:T(8,128)}, u32[]{:S(2)}) copy-start(f32[1,4,192,128]{3,2,1,0:T(8,128)} %param.18) | copy-start | bytes 1179652
  68.3 8.1 %collective-permute-start.8 = (f32[2,192,128]{2,1,0:T(8,128)}, f32[2,192,128]{2,1,0:T(8,128)S(1)}, u32[]{:S(2)}, u32[]{:S(2)}) collective-permute-start(f32[2,192,128]{2,1,0:T(8,128)} %get-tuple-element.30), channel_id=1, source_target_pairs={{1,0},{2,1},{3,2},{5,4},{6,5},{7,6},{9,8},{10,9},{11,10},{13,12},{... | collective-permute-start | bytes 589832 | tf_op jit(solution)/shard_map/ppermute | solution.py:25
  69.6 8.0 %collective-permute-start.9 = (f32[2,192,128]{2,1,0:T(8,128)}, f32[2,192,128]{2,1,0:T(8,128)S(1)}, u32[]{:S(2)}, u32[]{:S(2)}) collective-permute-start(f32[2,192,128]{2,1,0:T(8,128)} %get-tuple-element.31), channel_id=1, source_target_pairs={{0,1},{1,2},{2,3},{4,5},{5,6},{6,7},{8,9},{9,10},{10,11},{12,13},{... | collective-permute-start | bytes 589832 | tf_op jit(solution)/shard_map/ppermute | solution.py:22
  81.1 9.1 %collective-permute-start.10 = (f32[2,192,128]{2,1,0:T(8,128)S(1)}, f32[2,192,128]{2,1,0:T(8,128)S(1)}, u32[]{:S(2)}, u32[]{:S(2)}) collective-permute-start(f32[2,192,128]{2,1,0:T(8,128)S(1)} %get-tuple-element.28), channel_id=1, source_target_pairs={{1,0},{2,1},{3,2},{5,4},{6,5},{7,6},{9,8},{10,9},{11,10},{13,12},{... | collective-permute-start | bytes 589832 | tf_op jit(solution)/shard_map/ppermute | solution.py:25
  82.4 8.1 %collective-permute-start.11 = (f32[2,192,128]{2,1,0:T(8,128)S(1)}, f32[2,192,128]{2,1,0:T(8,128)S(1)}, u32[]{:S(2)}, u32[]{:S(2)}) collective-permute-start(f32[2,192,128]{2,1,0:T(8,128)S(1)} %get-tuple-element.29), channel_id=1, source_target_pairs={{0,1},{1,2},{2,3},{4,5},{5,6},{6,7},{8,9},{9,10},{10,11},{12,13},{... | collective-permute-start | bytes 589832 | tf_op jit(solution)/shard_map/ppermute | solution.py:22
  93.8 9.2 %collective-permute-start.12 = (f32[2,192,128]{2,1,0:T(8,128)}, f32[2,192,128]{2,1,0:T(8,128)}, u32[]{:S(2)}, u32[]{:S(2)}) collective-permute-start(f32[2,192,128]{2,1,0:T(8,128)} %get-tuple-element.26), channel_id=1, source_target_pairs={{1,0},{2,1},{3,2},{5,4},{6,5},{7,6},{9,8},{10,9},{11,10},{13,12},{... | collective-permute-start | bytes 589832 | tf_op jit(solution)/shard_map/ppermute | solution.py:25
  95.1 8.5 %collective-permute-start.13 = (f32[2,192,128]{2,1,0:T(8,128)}, f32[2,192,128]{2,1,0:T(8,128)}, u32[]{:S(2)}, u32[]{:S(2)}) collective-permute-start(f32[2,192,128]{2,1,0:T(8,128)} %get-tuple-element.27), channel_id=1, source_target_pairs={{0,1},{1,2},{2,3},{4,5},{5,6},{6,7},{8,9},{9,10},{10,11},{12,13},{... | collective-permute-start | bytes 589832 | tf_op jit(solution)/shard_map/ppermute | solution.py:22
  (8 other events, 12.2 us)
Sparse Core Ops, SparseCore 0:
  106.3 23.4 all-gather.2
